TPU v7x, 512 devices: a whole 4x8x8 slice. The times are simulated.
512 devices in a mesh: row: 16 (over x, y_hi), col: 32 (over z, y_lo, core).
Axes of the slice: x: 4, y: 8 (y_hi: 4, y_lo: 2; y = y_hi * 2 + y_lo), z: 8, core: 2. Of those that a mesh axis runs over, the one named last changes fastest.
Arguments:
- left_factor: float32 [8192, 512], P(('row', 'col')), may hold values from -0.0625 to 0.0625
- left_cotangent: float32 [8192, 512], P(('row', 'col')), may hold values from -80 to 80
- right_factor: float32 [24576, 512], P(('col', 'row')), may hold values from -0.0390625 to 0.0390625
- right_cotangent: float32 [24576, 512], P(('col', 'row')), may hold values from -80 to 80
- singular: float32 [512], replicated, may hold values from 0.5 to 2, as said below
- singular_cotangent: float32 [512], replicated, may hold values from -384 to 384
Outputs:
- matrix_cotangent: float32 [8192, 24576], P('row', 'col')
Inputs may be any that keep to these rules, and one draw needn't show every extreme that they name: `singular`: strictly decreasing; consecutive values differ by at least 0.75 / 512.
All inputs are finite; a program needn't handle non-finite values.
Results may differ from a plain program's by a relative error of at most 0.0003.
Values sent between devices are 32-bit elements; how exact they have to be, the bound alone decides.
No kernel may reach another device: no remote copies, remote signals or barrier semaphores. Data moves between devices by JAX's collectives and lax.ppermute only.
A program may use at most 64 MiB of HBM per device.

v0:
```python
import jax
import jax.numpy as jnp
from jax import lax
from jax.sharding import Mesh
from jax.sharding import PartitionSpec as P

ROW = ("x", "yh")
COL = ("z", "yl", "core")
ALL = ROW + COL
SIZES = (4, 4, 8, 2, 2)
HIGHEST = lax.Precision.HIGHEST


def dot(a, b, contract):
    return lax.dot_general(
        a, b, (contract, ((), ())), precision=HIGHEST, preferred_element_type=jnp.float32
    )


def gather(block, axis, size):
    copies = jnp.broadcast_to(block[None], (size,) + block.shape)
    return lax.all_to_all(copies, axis, 0, 0)


def partial_core(left, left_cot, right, right_cot, singular):
    squares = singular * singular
    spread = squares[None, :] - squares[:, None]
    size_k = singular.shape[0]
    diagonal = jnp.eye(size_k, dtype=jnp.bool_)
    divided = jnp.where(
        diagonal, jnp.float32(0.0), 1.0 / jnp.where(diagonal, jnp.float32(1.0), spread)
    )
    inverse = 1.0 / singular
    rows = ((0,), (0,))
    gram_left = dot(left, left_cot, rows)
    gram_left_t = dot(left_cot, left, rows)
    gram_right = dot(right, right_cot, rows)
    gram_right_t = dot(right_cot, right, rows)
    core = divided * (gram_left - gram_left_t) * singular[None, :]
    core = core + singular[:, None] * (divided * (gram_right - gram_right_t))
    return core - gram_left * inverse[None, :] - inverse[:, None] * gram_right_t


def local(left, left_cot, right, right_cot, singular, singular_cot):
    size_k = singular.shape[0]
    inverse = 1.0 / singular
    n_all = 512
    mine = partial_core(left, left_cot, right, right_cot, singular)
    spread_out = lax.all_to_all(mine.reshape(n_all, 4, 128), ALL, 0, 0)
    left_pair = jnp.concatenate([left, left_cot * inverse[None, :]], axis=1)
    right_pair = jnp.concatenate([right_cot * inverse[None, :], right], axis=1)
    lefts = lax.all_gather(left_pair, COL, axis=0, tiled=True)
    rights = lax.all_gather(right_pair, ROW, axis=0, tiled=True)
    row = jnp.sum(spread_out, axis=0)
    core = gather(row, ALL, n_all).reshape(size_k, size_k) + jnp.diag(singular_cot)
    last = ((1,), (1,))
    flat = dot(lefts, rights, last)
    panel = dot(lefts[:, :size_k], core, ((1,), (0,)))
    return flat + dot(panel, rights[:, size_k:], last)


def solution(mesh):
    fine = Mesh(mesh.devices.reshape(SIZES), ALL)
    placed = (
        P(ROW + COL, None),
        P(ROW + COL, None),
        P(COL + ROW, None),
        P(COL + ROW, None),
        P(),
        P(),
    )
    return jax.shard_map(local, mesh=fine, in_specs=placed, out_specs=P(ROW, COL), check_vma=False)
```

profile of v0, /device:TPU:1, one launch (start us, length us, event | category | flops | bytes accessed | tf_op | source)
XLA Modules:
  0.0 213.5 jit_solution(7543045240568604852)
XLA Ops:
  6.5 0.0 copy-start.7
  6.5 0.0 copy-start.2
  6.5 0.0 copy-start.3
  6.5 0.0 all-gather.3.cloned.1.call-start
  6.5 0.7 broadcast_divide_fusion
  7.3 0.8 broadcast_multiply_fusion.1
  8.1 1.4 pad_maximum_fusion.1
  9.5 0.0 all-gather.3.cloned.1.call-update
  9.5 0.0 all-gather.5.cloned.1.call-start
  9.5 0.9 broadcast_multiply_fusion
  10.4 1.6 pad_maximum_fusion
  12.0 0.0 all-gather.5.cloned.1.call-update
  12.1 1.8 fusion.11
  13.9 0.0 copy-done.2
  13.9 0.0 copy-done.3
  13.9 1.0 fusion.12
  14.9 0.0 copy-done.7
  14.9 0.0 copy-start.4
  14.9 0.0 copy-start.5
  14.9 1.1 fusion.8
  16.1 0.0 copy-done.4
  16.1 0.0 copy-done.5
  16.1 1.4 fusion.6
  17.5 0.4 copy.7
  17.9 55.0 %all_to_all.10 = f32[512,4,128]{2,1,0:T(4,128)S(1)} all-to-all(f32[512,4,128]{2,1,0:T(4,128)S(1)} %copy.7), channel_id=1, replica_groups=mesh['x'=4,'yh'=4,'z'=8,'yl'=2,'core'=2] {'x','yh','z','yl','core'}, dimensions={0} | all-to-all | bytes 2097152 | tf_op jit(solution)/shard_map/all_to_all | solution.py:49
  72.9 0.5 reduce_sum.9
  73.5 0.1 broadcast_in_dim.36
  73.6 0.0 copy-start.6
  73.6 42.8 %all_to_all.11 = f32[512,4,128]{2,1,0:T(4,128)S(1)} all-to-all(f32[512,4,128]{2,1,0:T(4,128)S(1)} %broadcast_in_dim.36), channel_id=1, replica_groups=mesh['x'=4,'yh'=4,'z'=8,'yl'=2,'core'=2] {'x','yh','z','yl','core'}, dimensions={0} | all-to-all | bytes 2097152 | tf_op jit(solution)/shard_map/all_to_all | solution.py:22
  116.4 0.4 copy.8
  116.8 0.0 copy-done.6
  116.8 0.1 bitcast_add_fusion
  116.9 0.0 all-gather.3.cloned.1.call-done
  116.9 0.0 copy-start.1
  116.9 4.2 %fusion.9 = f32[512,512]{1,0:T(8,128)} fusion(f32[512,512]{0,1:T(8,128)S(1)} %bitcast_add_fusion, f32[512,1024]{1,0:T(8,128)} %all-gather.3.cloned.1.call-done), kind=kOutput, calls=%fused_computation.12 | convolution fusion | flops 1610612736 | bytes 3145728 | tf_op jit(solution)/shard_map/dot_general | solution.py:15
  121.1 74.3 %all-gather.5.cloned.1.call-done = f32[768,1024]{1,0:T(8,128)} async-done(((f32[48,1024]{1,0:T(8,128)}), f32[768,1024]{1,0:T(8,128)}) %all-gather.5.cloned.1.call-update) | async-done | bytes 3145744 | tf_op jit(solution)/shard_map/all_gather | solution.py:53
  195.4 0.0 copy-start
  195.4 4.6 %fusion = f32[512,768]{1,0:T(8,128)S(1)} fusion(f32[512,512]{1,0:T(8,128)} %fusion.9, f32[768,1024]{1,0:T(8,128)} %all-gather.5.cloned.1.call-done), kind=kOutput, calls=%fused_computation | convolution fusion | flops 2415919104 | bytes 4194304 | tf_op jit(solution)/shard_map/dot_general | solution.py:15
  200.1 0.0 copy-done.1
  200.1 0.0 copy-done
  200.1 6.5 %convolution_add_fusion = f32[512,768]{1,0:T(8,128)} fusion(f32[512,768]{1,0:T(8,128)S(1)} %fusion, f32[512,1024]{1,0:T(8,128)S(1)} %copy-done.1, f32[768,1024]{1,0:T(8,128)S(1)} %copy-done), kind=kOutput, calls=%fused_computation.2 | convolution fusion | flops 4832231424 | bytes 8388608 | tf_op jit(solution)/shard_map/dot_general | solution.py:15
Async XLA Ops:
  6.5 8.4 %copy-start.7 = (f32[512]{0:T(512)S(1)}, f32[512]{0:T(512)}, u32[]{:S(2)}) copy-start(f32[512]{0:T(512)} %param.10) | copy-start | bytes 6148
  6.5 7.3 %copy-start.2 = (f32[48,512]{1,0:T(8,128)S(1)}, f32[48,512]{1,0:T(8,128)}, u32[]{:S(2)}) copy-start(f32[48,512]{1,0:T(8,128)} %param.9) | copy-start | bytes 294916
  6.5 7.3 %copy-start.3 = (f32[48,512]{1,0:T(8,128)S(1)}, f32[48,512]{1,0:T(8,128)}, u32[]{:S(2)}) copy-start(f32[48,512]{1,0:T(8,128)} %param.8) | copy-start | bytes 294916
  6.5 110.3 %all-gather.3.cloned.1.call-start = ((), (), s32[]{:S(2)}) async-start(), calls=%async_computation.2 | async-start | bytes 2162688 | tf_op jit(solution)/shard_map/all_gather | solution.py:52
  9.5 186.0 %all-gather.5.cloned.1.call-start = ((), (), s32[]{:S(2)}) async-start(), calls=%async_computation.3 | async-start | bytes 3342336 | tf_op jit(solution)/shard_map/all_gather | solution.py:53
  14.9 1.2 copy-start.4
  14.9 1.2 copy-start.5
  73.6 43.2 %copy-start.6 = (f32[512]{0:T(512)S(1)}, f32[512]{0:T(512)}, u32[]{:S(2)}) copy-start(f32[512]{0:T(512)} %param.11) | copy-start | bytes 6148
  116.9 83.2 %copy-start.1 = (f32[512,1024]{1,0:T(8,128)S(1)}, f32[512,1024]{1,0:T(8,128)}, u32[]{:S(2)}) copy-start(f32[512,1024]{1,0:T(8,128)} %all-gather.3.cloned.1.call-done) | copy-start | bytes 6291460
  195.4 4.6 %copy-start = (f32[768,1024]{1,0:T(8,128)S(1)}, f32[768,1024]{1,0:T(8,128)}, u32[]{:S(2)}) copy-start(f32[768,1024]{1,0:T(8,128)} %all-gather.5.cloned.1.call-done) | copy-start | bytes 9437188
Sparse Core Ops, SparseCore 0:
  9.6 101.7 all-gather.2
  114.4 80.9 all-gather.4
where the time goes:
time: 214 us; the launch traced here: 213 us
  blocking collectives  97.8 us (46%)
  waiting for transfers between devices  74.4 us (35%)
  matrix products  20.7 us (10%)
  between operations  13.6 us (6%)
  other arithmetic  6.06 us (3%)
    all_gather x1, waiting for transfers between devices, local(): rights = lax.all_gather(right_pair, ROW, axis=0, tiled=True)  74.3 us
    all_to_all x1, blocking collectives, local(): spread_out = lax.all_to_all(mine.reshape(n_all, 4, 128), ALL, 0, 0)  55 us
    all_to_all x1, blocking collectives, gather(): return lax.all_to_all(copies, axis, 0, 0)  42.8 us
    dot_general x7, matrix products, dot(): lax.dot_general(a, b, (contract, ((), ())), precision=HIGHEST, preferred_...  20.7 us
  transfers between devices with their start and end apart: 2, of which 1 were waited for; matrix products, arithmetic and copies ran while one was open for 6% of the time, Pallas kernels for 0%

commit v1 on v0

--- a/solution.py
+++ b/solution.py
@@ -50,7 +50,9 @@
     left_pair = jnp.concatenate([left, left_cot * inverse[None, :]], axis=1)
     right_pair = jnp.concatenate([right_cot * inverse[None, :], right], axis=1)
     lefts = lax.all_gather(left_pair, COL, axis=0, tiled=True)
-    rights = lax.all_gather(right_pair, ROW, axis=0, tiled=True)
+    rights = jnp.concatenate(
+        lax.all_to_all(jnp.stack([right_pair] * lax.axis_size(ROW)), ROW, 0, 0), axis=0
+    )
     row = jnp.sum(spread_out, axis=0)
     core = gather(row, ALL, n_all).reshape(size_k, size_k) + jnp.diag(singular_cot)
     last = ((1,), (1,))

time: 214 us -> 227 us (1.061)
  the two profiles are of different devices: /device:TPU:1 before, /device:TPU:39 now
where the time goes in v1:
time: 227 us
  waiting for transfers between devices  110 us (48%)
  blocking collectives  48.2 us (21%)
  starting transfers between devices  23.6 us (10%)
  matrix products  21.6 us (10%)
  between operations  13.6 us (6%)
  local copies, waits for them, and re-layouts  6.12 us (3%)
  other arithmetic  4.21 us (2%)
    all_gather x1, waiting for transfers between devices, local(): lefts = lax.all_gather(left_pair, COL, axis=0, tiled=True)  82.3 us
    all_to_all x1, blocking collectives, local(): spread_out = lax.all_to_all(mine.reshape(n_all, 4, 128), ALL, 0, 0)  48.2 us
    all_to_all x1, waiting for transfers between devices, gather(): return lax.all_to_all(copies, axis, 0, 0)  27.2 us
    dot_general x7, matrix products, dot(): lax.dot_general(a, b, (contract, ((), ())), precision=HIGHEST, preferred_...  21.6 us
    all_to_all x1, starting transfers between devices, gather(): return lax.all_to_all(copies, axis, 0, 0)  14.6 us
    all_to_all x1, starting transfers between devices, local(): lax.all_to_all(jnp.stack([right_pair] * lax.axis_size(ROW)), ROW, 0, 0)  8.78 us
  transfers between devices with their start and end apart: 3, of which 2 were waited for; matrix products, arithmetic and copies ran while one was open for 4% of the time, Pallas kernels for 0%

profile of v1, /device:TPU:39, one launch (start us, length us, event | category | flops | bytes accessed | tf_op | source)
XLA Modules:
  0.0 226.8 jit_solution(17379407837280669617)
XLA Ops:
  6.5 0.7 broadcast_divide_fusion
  7.2 2.0 fusion.12
  9.2 0.0 copy-start.4
  9.2 0.0 copy-start.5
  9.2 0.0 copy-start.7
  9.2 2.1 fusion.8
  11.3 0.0 copy-done.4
  11.4 0.0 copy-done.5
  11.4 1.0 fusion.11
  12.4 0.0 copy-done.7
  12.4 1.4 fusion.6
  13.8 0.4 copy.7
  14.2 48.2 %all_to_all.15 = f32[512,4,128]{2,1,0:T(4,128)S(1)} all-to-all(f32[512,4,128]{2,1,0:T(4,128)S(1)} %copy.7), channel_id=1, replica_groups=mesh['x'=4,'yh'=4,'z'=8,'yl'=2,'core'=2] {'x','yh','z','yl','core'}, dimensions={0} | all-to-all | bytes 2097152 | tf_op jit(solution)/shard_map/all_to_all | solution.py:49
  62.5 0.0 copy-start.2
  62.5 0.0 copy-start.3
  62.5 0.5 reduce_sum.9
  63.0 1.1 broadcast_in_dim.36
  64.1 14.6 %all-to-all-start.2 = ((f32[512,4,128]{2,1,0:T(4,128)}), f32[512,4,128]{2,1,0:T(4,128)S(1)}, u32[]{:S(2)}, u32[]{:S(2)}) async-start(f32[512,4,128]{2,1,0:T(4,128)} %broadcast_in_dim.36), calls=%async_computation.2 | async-start | bytes 2097152 | tf_op jit(solution)/shard_map/all_to_all | solution.py:22
  78.7 0.0 copy-done.2
  78.7 0.0 copy-done.3
  78.8 27.2 %all-to-all-done.2 = f32[512,4,128]{2,1,0:T(4,128)S(1)} async-done(((f32[512,4,128]{2,1,0:T(4,128)}), f32[512,4,128]{2,1,0:T(4,128)S(1)}, u32[]{:S(2)}, u32[]{:S(2)}) %all-to-all-start.2) | async-done | bytes 1048608 | tf_op jit(solution)/shard_map/all_to_all | solution.py:22
  105.9 0.0 copy-start.1
  106.0 2.0 stack.2
  108.0 0.0 copy-done.1
  108.0 8.8 %all-to-all-start = ((f32[16,48,1024]{2,1,0:T(8,128)}), f32[16,48,1024]{2,1,0:T(8,128)S(1)}, u32[]{:S(2)}, u32[]{:S(2)}) async-start(f32[16,48,1024]{2,1,0:T(8,128)} %stack.2), calls=%async_computation | async-start | bytes 6291456 | tf_op jit(solution)/shard_map/all_to_all | solution.py:54
  116.8 0.0 copy-start.6
  116.8 0.2 all-gather.2.cloned.1.call-start
  117.0 0.6 pad_maximum_fusion.1
  117.6 0.0 all-gather.2.cloned.1.call-update
  117.7 2.6 %copy.8 = f32[512,4,128]{0,2,1:T(8,128)} copy(f32[512,4,128]{2,1,0:T(4,128)} %copy-done.1) | data formatting | bytes 2097152 | tf_op jit(solution)/shard_map/all_to_all | solution.py:22
  120.2 0.0 copy-done.6
  120.2 2.3 %bitcast_add_fusion = f32[512,512]{0,1:T(8,128)} fusion(f32[512,4,128]{0,2,1:T(8,128)} %copy.8, f32[512]{0:T(512)S(1)} %copy-done.6), kind=kLoop, calls=%fused_computation.14 | loop fusion | flops 786432 | bytes 2099200 | tf_op jit(solution)/shard_map/add | solution.py:57
  122.5 82.3 %all-gather.2.cloned.1.call-done = f32[512,1024]{1,0:T(8,128)} async-done(((f32[16,1024]{1,0:T(8,128)}), f32[512,1024]{1,0:T(8,128)}) %all-gather.2.cloned.1.call-update) | async-done | bytes 2097168 | tf_op jit(solution)/shard_map/all_gather | solution.py:52
  204.9 4.4 %fusion.9 = f32[512,512]{1,0:T(8,128)} fusion(f32[512,512]{0,1:T(8,128)} %bitcast_add_fusion, f32[512,1024]{1,0:T(8,128)} %all-gather.2.cloned.1.call-done), kind=kOutput, calls=%fused_computation.12 | convolution fusion | flops 1610612736 | bytes 3145728 | tf_op jit(solution)/shard_map/dot_general | solution.py:15
  209.3 0.0 all-to-all-done
  209.3 0.0 copy-start
  209.3 4.1 %fusion = f32[512,768]{1,0:T(8,128)S(1)} fusion(f32[512,512]{1,0:T(8,128)} %fusion.9, f32[768,1024]{1,0:T(8,128)S(1)} %bitcast.16), kind=kOutput, calls=%fused_computation | convolution fusion | flops 2415919104 | bytes 4194304 | tf_op jit(solution)/shard_map/dot_general | solution.py:15
  213.4 0.0 copy-done
  213.4 6.5 %convolution_add_fusion = f32[512,768]{1,0:T(8,128)} fusion(f32[512,768]{1,0:T(8,128)S(1)} %fusion, f32[512,1024]{1,0:T(8,128)S(1)} %copy-done, f32[768,1024]{1,0:T(8,128)S(1)} %bitcast.17), kind=kOutput, calls=%fused_computation.2 | convolution fusion | flops 4832231424 | bytes 8388608 | tf_op jit(solution)/shard_map/dot_general | solution.py:15
  (3 shorter events, 0.0 us)
Async XLA Ops:
  9.2 2.2 copy-start.4
  9.2 2.2 copy-start.5
  9.2 3.2 %copy-start.7 = (f32[512]{0:T(512)S(1)}, f32[512]{0:T(512)}, u32[]{:S(2)}) copy-start(f32[512]{0:T(512)} %param.10) | copy-start | bytes 6148
  62.5 16.2 %copy-start.2 = (f32[48,512]{1,0:T(8,128)S(1)}, f32[48,512]{1,0:T(8,128)}, u32[]{:S(2)}) copy-start(f32[48,512]{1,0:T(8,128)} %param.9) | copy-start | bytes 294916
  62.5 16.3 %copy-start.3 = (f32[48,512]{1,0:T(8,128)S(1)}, f32[48,512]{1,0:T(8,128)}, u32[]{:S(2)}) copy-start(f32[48,512]{1,0:T(8,128)} %param.8) | copy-start | bytes 294916
  64.1 41.8 %all-to-all-start.2 = ((f32[512,4,128]{2,1,0:T(4,128)}), f32[512,4,128]{2,1,0:T(4,128)S(1)}, u32[]{:S(2)}, u32[]{:S(2)}) async-start(f32[512,4,128]{2,1,0:T(4,128)} %broadcast_in_dim.36), calls=%async_computation.2 | async-start | bytes 2097152 | tf_op jit(solution)/shard_map/all_to_all | solution.py:22
  105.9 2.0 copy-start.1
  108.0 101.3 %all-to-all-start = ((f32[16,48,1024]{2,1,0:T(8,128)}), f32[16,48,1024]{2,1,0:T(8,128)S(1)}, u32[]{:S(2)}, u32[]{:S(2)}) async-start(f32[16,48,1024]{2,1,0:T(8,128)} %stack.2), calls=%async_computation | async-start | bytes 6291456 | tf_op jit(solution)/shard_map/all_to_all | solution.py:54
  116.8 3.5 %copy-start.6 = (f32[512]{0:T(512)S(1)}, f32[512]{0:T(512)}, u32[]{:S(2)}) copy-start(f32[512]{0:T(512)} %param.11) | copy-start | bytes 6148
  116.8 88.1 %all-gather.2.cloned.1.call-start = ((), (), s32[]{:S(2)}) async-start(), calls=%async_computation.3 | async-start | bytes 2162688 | tf_op jit(solution)/shard_map/all_gather | solution.py:52
  209.3 4.1 %copy-start = (f32[512,1024]{1,0:T(8,128)S(1)}, f32[512,1024]{1,0:T(8,128)}, u32[]{:S(2)}) copy-start(f32[512,1024]{1,0:T(8,128)} %all-gather.2.cloned.1.call-done) | copy-start | bytes 6291460
Sparse Core Ops, SparseCore 0:
  119.7 85.1 all-gather.1
